TPU v7x, 128 devices: a whole 4x4x4 slice. The times are simulated.
128 devices in a mesh: pair: 2 (over core), virt: 64 (over z, y, x).
Axes of the slice: x: 4, y: 4, z: 4, core: 2. Of those that a mesh axis runs over, the one named last changes fastest.
Arguments:
- amplitudes: bfloat16 [512, 32768], P('virt', 'pair'), may hold values from -6 to 6
- integrals: bfloat16 [32768, 32768], P('virt', 'pair'), may hold values from -0.03125 to 0.03125
- cycle_integrals: bfloat16 [16384, 16384], P('pair', 'virt'), may hold values from -0.125 to 0.125
- virt_count: int32 [8], replicated, may hold values from 32 to 64, as said below
Outputs:
- ladder: bfloat16 [512, 32768], P(None, 'virt')
- cycle: bfloat16 [8192, 16384], P('pair', 'virt')
Inputs may be any that keep to these rules, and one draw needn't show every extreme that they name: `virt_count`: every irrep keeps at least half of its 64 slots; some irrep has all 64 and some has exactly half.
All inputs are finite; a program needn't handle non-finite values.
Results may differ from a plain program's by a relative error of at most 0.0049.
Values may be sent and summed in bfloat16 or wider, within the bound.
No kernel may reach another device: no remote copies, remote signals or barrier semaphores. Data moves between devices by JAX's collectives and lax.ppermute only.
A program may use at most 256 MiB of HBM per device.

v0:
```python
import jax
import jax.numpy as jnp
from jax import lax
from jax.sharding import PartitionSpec as P

VH = 64
OI = 16
OJ = 32


def irrep_sizes(virt_count, irrep_of):
    irrep_ids = jnp.arange(virt_count.shape[0], dtype=jnp.int32)
    return jnp.sum(
        jnp.where(irrep_of[:, None] == irrep_ids[None, :], virt_count[None, :], 0), axis=1
    )


def pair_mask(virt_count, first_pos, length, slot_width):
    position = first_pos + jnp.arange(length, dtype=jnp.int32)
    irrep_of = position // (slot_width * slot_width)
    slot_one = position // slot_width % slot_width
    slot_two = position % slot_width
    irrep_size = irrep_sizes(virt_count, irrep_of)
    return ((slot_one < irrep_size) & (slot_two < irrep_size)).astype(jnp.float32)


def slot_mask(virt_count, first_pos, length, slot_width):
    position = (first_pos + jnp.arange(length, dtype=jnp.int32)) % (
        virt_count.shape[0] * slot_width
    )
    irrep_of = position // slot_width
    slot_ids = position % slot_width
    return (slot_ids < irrep_sizes(virt_count, irrep_of)).astype(jnp.float32)


def body(amplitudes, integrals, cycle_integrals, virt_count):
    slot_width = VH
    irrep_total = virt_count.shape[0]
    group_width = irrep_total * slot_width
    pair_devs = lax.axis_size("pair")
    ab_count = integrals.shape[0]
    cd_count = integrals.shape[1]
    jb_count = cycle_integrals.shape[1]
    cd_first = lax.axis_index("pair") * cd_count
    ab_first = lax.axis_index("virt") * ab_count
    a_count = ab_count // slot_width
    per_irrep = slot_width * slot_width // ab_count
    masked = amplitudes * pair_mask(virt_count, cd_first, cd_count, slot_width)[None, :].astype(
        jnp.bfloat16
    )
    partial_sums = lax.dot_general(
        lax.all_gather(masked, "virt", axis=0, tiled=True),
        integrals,
        (((1,), (1,)), ((), ())),
        preferred_element_type=jnp.float32,
    )
    keep_pairs = pair_mask(virt_count, ab_first, ab_count, slot_width)[None, :]
    ladder_total = lax.psum(partial_sums, "pair")
    ladder = (ladder_total * keep_pairs).astype(jnp.bfloat16)
    keep_cols = slot_mask(virt_count, lax.axis_index("virt") * jb_count, jb_count, slot_width)[
        None, :
    ]
    pair_rows = ladder.reshape(OI, OJ, ab_count)
    k_local = OJ // pair_devs
    own_k = lax.dynamic_slice_in_dim(pair_rows, lax.axis_index("pair") * k_local, k_local, 1)[None]
    cycle_local = cycle_integrals.reshape(k_local, irrep_total, slot_width, jb_count)
    shards = lax.all_gather(own_k, "virt", axis=0, tiled=True)
    shard_count = shards.shape[0]
    irrep_ids = jnp.arange(shard_count, dtype=jnp.int32) * ab_count // (slot_width * slot_width)
    chosen = jnp.take(cycle_local, irrep_ids, axis=1)
    amp_block = shards.reshape(shard_count, OI, k_local, a_count, slot_width)
    pieces = jnp.einsum("sikac,kscj->siaj", amp_block, chosen, preferred_element_type=jnp.float32)
    full_term = jnp.transpose(
        pieces.reshape(irrep_total, per_irrep, OI, a_count, jb_count), (2, 0, 1, 3, 4)
    )
    full_term = full_term.reshape(OI * group_width, jb_count)
    summed = lax.psum_scatter(full_term, "pair", scatter_dimension=0, tiled=True)
    cycle = (summed * keep_cols).astype(jnp.bfloat16)
    return (ladder, cycle)


def solution(mesh):
    placed = (P("virt", "pair"), P("virt", "pair"), P("pair", "virt"), P())
    return jax.shard_map(
        body,
        mesh=mesh,
        in_specs=placed,
        out_specs=(P(None, "virt"), P("pair", "virt")),
        check_vma=False,
    )
```

profile of v0, /device:TPU:1, one launch (start us, length us, event | category | flops | bytes accessed | tf_op | source)
XLA Modules:
  0.0 376.8 jit_solution(9450437816914688675)
XLA Ops:
  7.2 0.0 all-gather.4.cloned.1.call-start
  7.3 0.9 select_reduce_fusion
  8.2 0.1 convert_convert_fusion
  8.3 1.7 broadcast_multiply_fusion
  10.0 0.0 all-gather.4.cloned.1.call-update
  10.0 0.0 copy-start.1
  10.0 0.0 all-reduce.2.cloned.1.call-start
  10.1 109.0 %all-gather.4.cloned.1.call-done = bf16[512,16384]{1,0:T(8,128)(2,1)} async-done(((bf16[8,16384]{1,0:T(8,128)(2,1)}), bf16[512,16384]{1,0:T(8,128)(2,1)}) %all-gather.4.cloned.1.call-update) | async-done | bytes 16777232 | tf_op jit(solution)/shard_map/all_gather | solution.py:52
  119.1 18.0 %fusion.26 = f32[512,512]{1,0:T(8,128)} fusion(bf16[512,16384]{1,0:T(8,128)(2,1)} %all-gather.4.cloned.1.call-done, bf16[512,16384]{1,0:T(8,128)(2,1)} %param.5), kind=kOutput, calls=%fused_computation.87 | convolution fusion | flops 8589934592 | bytes 34603008 | tf_op jit(solution)/shard_map/dot_general | solution.py:51
  137.1 0.0 all-reduce.2.cloned.1.call-update
  137.1 0.0 all-gather.6.cloned.1.call-start
  137.2 0.0 copy-done.1
  137.2 0.1 select_reduce_fusion.1
  137.3 25.1 %all-reduce.2.cloned.1.call-done = f32[512,512]{1,0:T(8,128)} async-done(((f32[512,512]{1,0:T(8,128)}), f32[512,512]{1,0:T(8,128)}) %all-reduce.2.cloned.1.call-update) | async-done | bytes 1048592 | tf_op jit(solution)/shard_map/psum | solution.py:58
  162.4 1.3 multiply_convert_fusion.1
  163.8 0.0 copy-start
  163.8 0.8 constant_dynamic-slice_fusion
  164.6 0.0 all-gather.6.cloned.1.call-update
  164.6 0.0 reduce-scatter.2.cloned.1.call-start
  164.7 14.7 %gather_fusion = bf16[64,16,64,256]{3,2,1,0:T(8,128)(2,1)} fusion(bf16[16,8,64,256]{3,2,1,0:T(8,128)(2,1)} %bitcast.21, s32[1024]{0:T(1024)S(1)} %pad_clamp_fusion), kind=kCustom, calls=%fused_computation | custom fusion | bytes 67109120 | tf_op jit(solution)/shard_map/jit(_take)/gather | solution.py:70
  179.4 0.0 copy-done
  179.4 92.2 %all-gather.6.cloned.1.call-done = bf16[1024,16,512]{2,1,0:T(8,128)(2,1)} async-done(((bf16[16,16,512]{2,1,0:T(8,128)(2,1)}), bf16[1024,16,512]{2,1,0:T(8,128)(2,1)}) %all-gather.6.cloned.1.call-update) | async-done | bytes 16777232 | tf_op jit(solution)/shard_map/all_gather | solution.py:67
  271.6 41.3 %reshape.281 = bf16[64,16,16,8,64]{4,3,2,1,0:T(8,128)(2,1)} reshape(bf16[1024,16,512]{2,1,0:T(8,128)(2,1)} %all-gather.6.cloned.1.call-done) | data formatting | bytes 33554432 | tf_op jit(solution)/shard_map/reshape | solution.py:71
  312.9 25.9 %fusion = f32[64,16,8,256,1]{3,2,4,1,0:T(8,128)} fusion(bf16[64,16,16,8,64]{4,3,2,1,0:T(8,128)(2,1)} %reshape.281, bf16[64,16,64,256]{3,2,1,0:T(8,128)(2,1)} %gather_fusion, pred[64]{0:T(512)(128)(4,1)S(1)} %compare_and_fusion), kind=kOutput, calls=%fused_computation.1 | convolution fusion | flops 4311744512 | bytes 58720320 | tf_op jit(solution)/shard_map/sikac,kscj->siaj/dot_general | solution.py:72
  338.8 7.9 %copy.8 = f32[16,8,8,8,256]{4,3,2,1,0:T(8,128)} copy(f32[16,8,8,8,256]{4,3,0,2,1:T(8,128)} %bitcast.23) | data formatting | bytes 16777216 | tf_op jit(solution)/shard_map/transpose | solution.py:73
  346.7 0.0 reduce-scatter.2.cloned.1.call-update
  346.8 0.1 select_reduce_fusion.2
  346.9 19.5 %reduce-scatter.2.cloned.1.call-done = f32[4096,256]{1,0:T(8,128)} async-done(((f32[8192,256]{1,0:T(8,128)}), f32[4096,256]{1,0:T(8,128)}) %reduce-scatter.2.cloned.1.call-update) | async-done | bytes 4194320 | tf_op jit(solution)/shard_map/reduce_scatter | solution.py:77
  366.4 3.8 %multiply_convert_fusion = bf16[4096,256]{1,0:T(8,128)(2,1)} fusion(f32[4096,256]{1,0:T(8,128)} %reduce-scatter.2.cloned.1.call-done, f32[256]{0:T(256)S(1)} %compare_convert_fusion), kind=kLoop, calls=%fused_computation.6 | loop fusion | flops 2097152 | bytes 6292480 | tf_op jit(solution)/shard_map/convert_element_type | solution.py:78
  (8 shorter events, 0.2 us)
Async XLA Ops:
  7.2 111.9 %all-gather.4.cloned.1.call-start = ((), (), s32[]{:S(2)}) async-start(), calls=%async_computation.1 | async-start | bytes 17039360 | tf_op jit(solution)/shard_map/all_gather | solution.py:52
  10.0 127.2 %copy-start.1 = (s32[8]{0:T(128)S(1)}, s32[8]{0:T(128)}, u32[]{:S(2)}) copy-start(s32[8]{0:T(128)} %param.7) | copy-start | bytes 100
  10.0 152.4 %all-reduce.2.cloned.1.call-start = ((), (), s32[]{:S(2)}) async-start(), calls=%async_computation.2 | async-start | bytes 2097152 | tf_op jit(solution)/shard_map/psum | solution.py:58
  137.1 134.5 %all-gather.6.cloned.1.call-start = ((), (), s32[]{:S(2)}) async-start(), calls=%async_computation.4 | async-start | bytes 17039360 | tf_op jit(solution)/shard_map/all_gather | solution.py:67
  163.8 15.6 %copy-start = (bf16[512,512]{1,0:T(8,128)(2,1)}, bf16[512,512]{1,0:T(8,128)(2,1)S(1)}, u32[]{:S(2)}) copy-start(bf16[512,512]{1,0:T(8,128)(2,1)S(1)} %multiply_convert_fusion.1) | copy-start | bytes 1572868
  164.6 201.8 %reduce-scatter.2.cloned.1.call-start = ((), (), s32[]{:S(2)}) async-start(), calls=%async_computation.3 | async-start | bytes 12582912 | tf_op jit(solution)/shard_map/reduce_scatter | solution.py:77
Sparse Core Ops, SparseCore 0:
  11.4 107.5 all-gather.3
  137.2 25.1 all-reduce.1
  166.3 105.2 all-gather.5
  346.9 19.4 reduce-scatter.1
where the time goes:
time: 378 us; the launch traced here: 377 us
  waiting for transfers between devices  246 us (65%)
  local copies, waits for them, and re-layouts  64.7 us (17%)
  matrix products  43.9 us (12%)
  between operations  13.8 us (4%)
  other arithmetic  8.2 us (2%)
    all_gather x1, waiting for transfers between devices, body(): lax.all_gather(masked, 'virt', axis=0, tiled=True)  109 us
    all_gather x1, waiting for transfers between devices, body(): shards = lax.all_gather(own_k, 'virt', axis=0, tiled=True)  92.2 us
    reshape x1, local copies, waits for them, and re-layouts, body(): amp_block = shards.reshape(shard_count, OI, k_local, a_count, slot_width)  41.3 us
    dot_general x1, matrix products, body(): jnp.einsum('sikac,kscj->siaj', amp_block, chosen, preferred_element_type=...  25.9 us
    psum x1, waiting for transfers between devices, body(): ladder_total = lax.psum(partial_sums, 'pair')  25.1 us
    reduce_scatter x1, waiting for transfers between devices, body(): lax.psum_scatter(full_term, 'pair', scatter_dimension=0, tiled=True)  19.5 us
    dot_general x1, matrix products, body(): lax.dot_general(lax.all_gather(masked, 'virt', axis=0, tiled=True), integ...  18 us
    gather x1, local copies, waits for them, and re-layouts, body(): chosen = jnp.take(cycle_local, irrep_ids, axis=1)  14.7 us
  transfers between devices with their start and end apart: 4, of which 4 were waited for; matrix products, arithmetic and copies ran while one was open for 4% of the time, Pallas kernels for 0%

commit v1 on v0

--- a/solution.py
+++ b/solution.py
@@ -55,7 +55,8 @@
         preferred_element_type=jnp.float32,
     )
     keep_pairs = pair_mask(virt_count, ab_first, ab_count, slot_width)[None, :]
-    ladder_total = lax.psum(partial_sums, "pair")
+    replace_forms = lambda block_in: lax.all_gather(block_in, "pair").sum(axis=0)
+    ladder_total = replace_forms(partial_sums)
     ladder = (ladder_total * keep_pairs).astype(jnp.bfloat16)
     keep_cols = slot_mask(virt_count, lax.axis_index("virt") * jb_count, jb_count, slot_width)[
         None, :

time: 378 us -> 366 us (0.968)
  waiting for transfers between devices: 246 us -> 232 us
    psum x1 -> x0, waiting for transfers between devices: 25.1 us -> none  [body(): ladder_total = lax.psum(partial_sums, 'pair')]
    all_gather x0 -> x1, waiting for transfers between devices: none -> 13.2 us  [body(): lax.all_gather(block_in, 'pair').sum(axis=0)]
where the time goes in v1:
time: 366 us; the launch traced here: 364 us
  waiting for transfers between devices  232 us (63%)
  local copies, waits for them, and re-layouts  63.9 us (17%)
  matrix products  43.9 us (12%)
  between operations  13.8 us (4%)
  other arithmetic  10.4 us (3%)
    all_gather x1, waiting for transfers between devices, body(): lax.all_gather(masked, 'virt', axis=0, tiled=True)  109 us
    all_gather x1, waiting for transfers between devices, body(): shards = lax.all_gather(own_k, 'virt', axis=0, tiled=True)  91.3 us
    reshape x1, local copies, waits for them, and re-layouts, body(): amp_block = shards.reshape(shard_count, OI, k_local, a_count, slot_width)  41.3 us
    dot_general x1, matrix products, body(): jnp.einsum('sikac,kscj->siaj', amp_block, chosen, preferred_element_type=...  25.9 us
    reduce_scatter x1, waiting for transfers between devices, body(): lax.psum_scatter(full_term, 'pair', scatter_dimension=0, tiled=True)  18.6 us
    dot_general x1, matrix products, body(): lax.dot_general(lax.all_gather(masked, 'virt', axis=0, tiled=True), integ...  18 us
    gather x1, local copies, waits for them, and re-layouts, body(): chosen = jnp.take(cycle_local, irrep_ids, axis=1)  14.7 us
    all_gather x1, waiting for transfers between devices, body(): lax.all_gather(block_in, 'pair').sum(axis=0)  13.2 us
  transfers between devices with their start and end apart: 4, of which 4 were waited for; matrix products, arithmetic and copies ran while one was open for 4% of the time, Pallas kernels for 0%

profile of v1, /device:TPU:1, one launch (start us, length us, event | category | flops | bytes accessed | tf_op | source)
XLA Modules:
  0.0 364.5 jit_solution(6908478136303853208)
XLA Ops:
  7.2 0.0 all-gather.6.cloned.1.call-start
  7.3 0.9 select_reduce_fusion
  8.2 0.1 convert_convert_fusion
  8.3 1.7 broadcast_multiply_fusion
  10.0 0.0 all-gather.6.cloned.1.call-update
  10.0 0.0 copy-start
  10.0 0.0 all-gather.8.cloned.1.call-start
  10.1 109.0 %all-gather.6.cloned.1.call-done = bf16[512,16384]{1,0:T(8,128)(2,1)} async-done(((bf16[8,16384]{1,0:T(8,128)(2,1)}), bf16[512,16384]{1,0:T(8,128)(2,1)}) %all-gather.6.cloned.1.call-update) | async-done | bytes 16777232 | tf_op jit(solution)/shard_map/all_gather | solution.py:52
  119.1 18.0 %fusion.27 = f32[512,512]{1,0:T(8,128)} fusion(bf16[512,16384]{1,0:T(8,128)(2,1)} %all-gather.6.cloned.1.call-done, bf16[512,16384]{1,0:T(8,128)(2,1)} %param.5), kind=kOutput, calls=%fused_computation.88 | convolution fusion | flops 8589934592 | bytes 34603008 | tf_op jit(solution)/shard_map/dot_general | solution.py:51
  137.1 0.0 all-gather.8.cloned.1.call-update
  137.1 0.0 all-gather.10.cloned.1.call-start
  137.2 0.0 copy-done
  137.2 0.1 select_reduce_fusion.1
  137.3 13.2 %all-gather.8.cloned.1.call-done = f32[1024,512]{1,0:T(8,128)} async-done(((f32[512,512]{1,0:T(8,128)}), f32[1024,512]{1,0:T(8,128)}) %all-gather.8.cloned.1.call-update) | async-done | bytes 2097168 | tf_op jit(solution)/shard_map/all_gather | solution.py:58
  150.5 1.9 reduce_sum.39
  152.4 0.8 fusion.5
  153.2 0.0 all-gather.10.cloned.1.call-update
  153.2 0.0 reduce-scatter.2.cloned.1.call-start
  153.3 14.7 %gather_fusion = bf16[64,16,64,256]{3,2,1,0:T(8,128)(2,1)} fusion(bf16[16,8,64,256]{3,2,1,0:T(8,128)(2,1)} %bitcast.22, s32[1024]{0:T(1024)S(1)} %pad_clamp_fusion), kind=kCustom, calls=%fused_computation | custom fusion | bytes 67109120 | tf_op jit(solution)/shard_map/jit(_take)/gather | solution.py:71
  168.0 91.3 %all-gather.10.cloned.1.call-done = bf16[1024,16,512]{2,1,0:T(8,128)(2,1)} async-done(((bf16[16,16,512]{2,1,0:T(8,128)(2,1)}), bf16[1024,16,512]{2,1,0:T(8,128)(2,1)}) %all-gather.10.cloned.1.call-update) | async-done | bytes 16777232 | tf_op jit(solution)/shard_map/all_gather | solution.py:68
  259.3 41.3 %reshape.284 = bf16[64,16,16,8,64]{4,3,2,1,0:T(8,128)(2,1)} reshape(bf16[1024,16,512]{2,1,0:T(8,128)(2,1)} %all-gather.10.cloned.1.call-done) | data formatting | bytes 33554432 | tf_op jit(solution)/shard_map/reshape | solution.py:72
  300.6 25.9 %fusion = f32[64,16,8,256,1]{3,2,4,1,0:T(8,128)} fusion(bf16[64,16,16,8,64]{4,3,2,1,0:T(8,128)(2,1)} %reshape.284, bf16[64,16,64,256]{3,2,1,0:T(8,128)(2,1)} %gather_fusion, pred[64]{0:T(512)(128)(4,1)S(1)} %compare_and_fusion), kind=kOutput, calls=%fused_computation.1 | convolution fusion | flops 4311744512 | bytes 58720320 | tf_op jit(solution)/shard_map/sikac,kscj->siaj/dot_general | solution.py:73
  326.5 7.9 %copy.8 = f32[16,8,8,8,256]{4,3,2,1,0:T(8,128)} copy(f32[16,8,8,8,256]{4,3,0,2,1:T(8,128)} %bitcast.24) | data formatting | bytes 16777216 | tf_op jit(solution)/shard_map/transpose | solution.py:74
  334.4 0.0 reduce-scatter.2.cloned.1.call-update
  334.5 0.1 select_reduce_fusion.2
  334.6 0.9 multiply_convert_fusion.1
  335.5 18.6 %reduce-scatter.2.cloned.1.call-done = f32[4096,256]{1,0:T(8,128)} async-done(((f32[8192,256]{1,0:T(8,128)}), f32[4096,256]{1,0:T(8,128)}) %reduce-scatter.2.cloned.1.call-update) | async-done | bytes 4194320 | tf_op jit(solution)/shard_map/reduce_scatter | solution.py:78
  354.1 3.8 %multiply_convert_fusion = bf16[4096,256]{1,0:T(8,128)(2,1)} fusion(f32[4096,256]{1,0:T(8,128)} %reduce-scatter.2.cloned.1.call-done, f32[256]{0:T(256)S(1)} %compare_convert_fusion), kind=kLoop, calls=%fused_computation.6 | loop fusion | flops 2097152 | bytes 6292480 | tf_op jit(solution)/shard_map/convert_element_type | solution.py:79
  (8 shorter events, 0.2 us)
Async XLA Ops:
  7.2 111.9 %all-gather.6.cloned.1.call-start = ((), (), s32[]{:S(2)}) async-start(), calls=%async_computation.1 | async-start | bytes 17039360 | tf_op jit(solution)/shard_map/all_gather | solution.py:52
  10.0 127.2 %copy-start = (s32[8]{0:T(128)S(1)}, s32[8]{0:T(128)}, u32[]{:S(2)}) copy-start(s32[8]{0:T(128)} %param.7) | copy-start | bytes 100
  10.0 140.5 %all-gather.8.cloned.1.call-start = ((), (), s32[]{:S(2)}) async-start(), calls=%async_computation.3 | async-start | bytes 3145728 | tf_op jit(solution)/shard_map/all_gather | solution.py:58
  137.1 122.2 %all-gather.10.cloned.1.call-start = ((), (), s32[]{:S(2)}) async-start(), calls=%async_computation.4 | async-start | bytes 17039360 | tf_op jit(solution)/shard_map/all_gather | solution.py:68
  153.2 200.9 %reduce-scatter.2.cloned.1.call-start = ((), (), s32[]{:S(2)}) async-start(), calls=%async_computation.2 | async-start | bytes 12582912 | tf_op jit(solution)/shard_map/reduce_scatter | solution.py:78
Sparse Core Ops, SparseCore 0:
  11.4 107.5 all-gather.5
  137.2 13.2 all-gather.7
  154.0 105.2 all-gather.9
  334.6 19.4 reduce-scatter.1
